TPU v7x, 32 devices: a whole 2x2x4 slice. The times are simulated.
32 devices in a mesh: cell: 8 (over z, y), dp: 4 (over x, core).
Axes of the slice: x: 2, y: 2, z: 4, core: 2. Of those that a mesh axis runs over, the one named last changes fastest.
Arguments:
- ensemble: bfloat16 [32768, 512], P('cell'), may hold values from -6 to 6
- response_estimates: float32 [4, 256, 512], P('dp', 'cell'), may hold values from -11 to 11
- observed: float32 [4, 256, 512], P('dp', 'cell'), may hold values from -12 to 12
- obs_std: float32 [4, 256], P('dp', 'cell'), may hold values from 0.2 to 0.5
- threshold: bfloat16 [4, 256], P('dp', 'cell'), may hold values from 0.019897461 to 0.119628906
Outputs:
- updated: float32 [32768, 512], P('cell', 'dp')
- mismatch: float32 [], replicated
All inputs are finite; a program needn't handle non-finite values.
Results may differ from a plain program's by a relative error of at most 0.0082.
Values may be sent and summed in bfloat16 or wider, within the bound.
A program may use at most 128 MiB of HBM per device.

v0:
```python
import math

import jax
import jax.numpy as jnp
from jax import lax
from jax.experimental import pallas as pl
from jax.experimental.pallas import tpu as pltpu
from jax.sharding import PartitionSpec as P

inflation = 4.0
LANES = 128
CHECK_EVERY = 3
F32 = jnp.float32
BF16 = jnp.bfloat16


def pieces(x):
    out = []
    for _ in range(3):
        part = lax.reduce_precision(x, 8, 7)
        out.append(part.astype(BF16))
        x = x - part
    return out


def joined(parts, at):
    return (
        parts[:, at].astype(F32) + parts[:, at + 1].astype(F32) + parts[:, at + 2].astype(F32)
    )


def split2(x):
    high = x.astype(BF16)
    return high, (x - high.astype(F32)).astype(BF16)


def tdot(a, b):
    return lax.dot_general(a, b, (((0,), (0,)), ((), ())), preferred_element_type=F32)


def solve_kernel(limit_steps, unit, innovation, ratio, carry, out, s2, a2, work, x, r, p, norms):
    nd, ne = unit.shape
    cols = innovation.shape[1]
    high, low = split2(unit[...].astype(F32) * ratio[...])
    s2[:nd, :] = high
    s2[nd:, :] = low
    cross = tdot(high, low)
    work[...] = cross + cross.T
    work[...] += tdot(high, high)
    for first in range(0, ne, cols):
        rows = pl.ds(first, cols)
        across = lax.broadcasted_iota(jnp.int32, (cols, ne), 1)
        down = lax.broadcasted_iota(jnp.int32, (cols, ne), 0) + first
        block = work[rows, :] + jnp.where(across == down, 1.0, 0.0)
        a_high, a_low = split2(block)
        a2[rows, :] = a_high
        a2[pl.ds(ne + first, cols), :] = a_low
    inn = innovation[...]
    rhs = tdot(high, inn) + tdot(low, inn)
    inn32 = inn.astype(F32)
    goal = jnp.sum(inn32 * inn32, axis=0, keepdims=True) * (2.0**-30)
    x[...] = jnp.zeros_like(x)
    r[...] = rhs
    p[...] = rhs
    rr0 = jnp.sum(rhs * rhs, axis=0, keepdims=True)
    norms[0:1, :] = rr0
    norms[1:2, :] = goal

    def more(state):
        step, worst = state
        return jnp.logical_and(step < limit_steps, worst > 0.0)

    def block(state):
        step, _ = state
        rr = norms[0:1, :]
        for _ in range(CHECK_EVERY):
            p_now = p[...]
            p_high, p_low = split2(p_now)
            both = jnp.dot(
                a2[...], jnp.concatenate([p_high, p_low], axis=1), preferred_element_type=F32
            )
            q = (both[:ne, :cols] + both[:ne, cols:]) + (both[ne:, :cols] + both[ne:, cols:])
            pq = jnp.sum(p_now * q, axis=0, keepdims=True)
            alpha = jnp.where(pq > 0.0, rr / jnp.where(pq > 0.0, pq, 1.0), 0.0)
            x[...] = x[...] + alpha * p_now
            r_new = r[...] - alpha * q
            r[...] = r_new
            rr_new = jnp.sum(r_new * r_new, axis=0, keepdims=True)
            beta = jnp.where(rr > 0.0, rr_new / jnp.where(rr > 0.0, rr, 1.0), 0.0)
            p[...] = r_new + beta * p_now
            rr = rr_new
        norms[0:1, :] = rr
        return step + CHECK_EVERY, jnp.max(rr - norms[1:2, :])

    lax.while_loop(more, block, (jnp.int32(0), jnp.max(rr0 - goal)))
    x_high, x_low = split2(x[...])
    both = jnp.dot(s2[...], jnp.concatenate([x_high, x_low], axis=1), preferred_element_type=F32)
    fitted = (both[:nd, :cols] + both[:nd, cols:]) + (both[nd:, :cols] + both[nd:, cols:])
    out[...] = ((inn32 - fitted) * carry[...]).astype(BF16)


def solve(unit, innovation, ratio, carry):
    nd, ne = unit.shape
    cols = innovation.shape[1]
    vmem = pl.BlockSpec(memory_space=pltpu.VMEM)
    return pl.pallas_call(
        lambda *refs: solve_kernel(8 * ne, *refs),
        out_shape=jax.ShapeDtypeStruct((nd, cols), BF16),
        in_specs=[vmem] * 4,
        out_specs=vmem,
        scratch_shapes=[
            pltpu.VMEM((2 * nd, ne), BF16),
            pltpu.VMEM((2 * ne, ne), BF16),
            pltpu.VMEM((ne, ne), F32),
            pltpu.VMEM((ne, cols), F32),
            pltpu.VMEM((ne, cols), F32),
            pltpu.VMEM((ne, cols), F32),
            pltpu.VMEM((8, cols), F32),
        ],
        compiler_params=pltpu.CompilerParams(vmem_limit_bytes=40 * 2**20),
        name="solve",
    )(unit, innovation, ratio, carry)


def per_device(ensemble, response_estimates, observed, obs_std, threshold):
    ne = ensemble.shape[1]
    forecast = response_estimates[0]
    observe = observed[0]
    noise_root = obs_std[0] * math.sqrt(inflation)
    deviation = forecast - jnp.mean(forecast, axis=1, keepdims=True)
    data_scale = jnp.sqrt(jnp.mean(deviation * deviation, axis=1) + 1e-06)
    unit_data = (deviation / (data_scale[:, None] * math.sqrt(ne))).astype(BF16)
    ratio = data_scale * math.sqrt(ne) / (noise_root * math.sqrt(ne - 1.0))
    carry = data_scale / noise_root
    innovation = (observe - forecast) / noise_root[:, None]
    squares = jnp.sum(innovation * innovation, axis=1)
    meta = jnp.stack(
        pieces(ratio) + pieces(carry) + pieces(squares) + [threshold[0].astype(BF16)], axis=1
    )
    meta = jnp.pad(meta, ((0, 0), (0, LANES - meta.shape[1])))
    payload = jnp.concatenate([unit_data, innovation.astype(BF16), meta], axis=1)
    whole = lax.all_gather(payload, ("cell", "dp"), axis=0, tiled=True)
    nd = whole.shape[0]
    column_count = ne // lax.axis_size("dp")
    first_col = lax.axis_index("dp") * column_count
    unit_all = whole[:, :ne]
    own_innovation = lax.dynamic_slice_in_dim(whole, ne + first_col, column_count, 1)
    parts = whole[:, 2 * ne :]
    mismatch = jnp.sum(joined(parts, 6)) / (nd * ne)
    carried = solve(
        unit_all, own_innovation, joined(parts, 0)[:, None], joined(parts, 3)[:, None]
    )
    limit = parts[:, 9].astype(F32)

    values = ensemble.astype(F32)
    anomaly = values - jnp.mean(values, axis=1, keepdims=True)
    cell_scale = jnp.sqrt(jnp.mean(anomaly * anomaly, axis=1) + 1e-06)
    unit_cells = (anomaly / (cell_scale[:, None] * math.sqrt(ne))).astype(BF16)
    correlate = lax.dot_general(
        unit_cells, unit_all, (((1,), (1,)), ((), ())), preferred_element_type=F32
    )
    square = correlate * correlate
    weighted = (square / (square + (limit * limit)[None, :]) * correlate).astype(BF16)
    increment = jnp.dot(weighted, carried, preferred_element_type=F32)
    own_values = lax.dynamic_slice_in_dim(values, first_col, column_count, 1)
    updated = own_values + cell_scale[:, None] * (ne / (ne - 1.0)) * increment
    return (updated, mismatch)


def solution(mesh):
    return jax.shard_map(
        per_device,
        mesh=mesh,
        in_specs=(
            P("cell", None),
            P("dp", "cell", None),
            P("dp", "cell", None),
            P("dp", "cell"),
            P("dp", "cell"),
        ),
        out_specs=(P("cell", "dp"), P()),
        check_vma=False,
    )
```

profile of v0, /device:TPU:11, one launch (start us, length us, event | category | flops | bytes accessed | tf_op | source)
XLA Modules:
  0.0 153.2 jit_solution(15386952156932527990)
XLA Ops:
  7.2 0.0 all-gather.2.cloned.1.call-start
  7.2 1.0 reduce_sum.58
  8.2 1.0 multiply_reduce_fusion.3
  9.2 0.7 bitcast_divide_fusion
  9.9 0.7 multiply_bitcast_fusion.1
  10.5 0.7 copy.29
  11.3 0.1 copy.24
  11.4 0.1 copy.23
  11.5 0.1 copy.21
  11.6 1.0 fusion.28
  12.5 0.1 multiply_reduce_fusion.2
  12.6 0.1 copy.26
  12.7 0.1 copy.27
  12.9 0.1 stack.2
  13.0 0.6 fusion.15
  13.6 0.0 all-gather.2.cloned.1.call-update
  13.7 6.6 %convert_element_type.151 = f32[4096,512]{1,0:T(8,128)} convert(bf16[4096,512]{1,0:T(8,128)(2,1)} %param.5) | non-fusion elementwise | flops 2097152 | bytes 12582912 | tf_op jit(solution)/shard_map/convert_element_type | solution.py:155
  20.3 2.8 %convert_reduce_fusion = f32[4096]{0:T(1024)S(1)} fusion(bf16[4096,512]{1,0:T(8,128)(2,1)} %param.5), kind=kLoop, calls=%fused_computation.7 | loop fusion | flops 4190208 | bytes 4210688 | tf_op jit(solution)/shard_map/reduce_sum | solution.py:156
  23.1 3.4 %multiply_reduce_fusion = f32[4096]{0:T(1024)S(1)} fusion(bf16[4096,512]{1,0:T(8,128)(2,1)} %param.5, f32[4096]{0:T(1024)S(1)} %broadcast_multiply_fusion), kind=kLoop, calls=%fused_computation.4 | loop fusion | flops 8384512 | bytes 4227072 | tf_op jit(solution)/shard_map/reduce_sum | solution.py:157
  26.5 45.0 %all-gather.2.cloned.1.call-done = bf16[1024,1152]{1,0:T(8,128)(2,1)} async-done(((bf16[32,1152]{1,0:T(8,128)(2,1)}), bf16[1024,1152]{1,0:T(8,128)(2,1)}) %all-gather.2.cloned.1.call-update) | async-done | bytes 2359312 | tf_op jit(solution)/shard_map/all_gather | solution.py:142
  71.5 4.2 %add_reduce_fusion = (f32[]{:T(128)}, f32[1024]{0:T(1024)S(1)}, f32[1024,1]{1,0:T(8,128)S(1)}, f32[1024,1]{1,0:T(8,128)S(1)}) fusion(bf16[1024,1152]{1,0:T(8,128)(2,1)} %all-gather.2.cloned.1.call-done), kind=kLoop, calls=%fused_computation.11 | loop fusion | flops 18431 | bytes 32772 | tf_op jit(solution)/shard_map/reduce_sum | solution.py:149
  76.4 1.3 slice.55.refs_0_
  77.7 1.0 constant_dynamic-slice_fusion.refs_1_
  78.7 55.7 %solve.1 = bf16[1024,128]{1,0:T(8,128)(2,1)S(1)} custom-call(bf16[1024,512]{1,0:T(8,128)(2,1)S(1)} %slice.55.refs_0_, bf16[1024,128]{1,0:T(8,128)(2,1)S(1)} %constant_dynamic-slice_fusion.refs_1_, f32[1024,1]{1,0:T(8,128)S(1)} %get-tuple-element.6.refs_2_, f32[1024,1]{1,0:T(8,128)S(1)} %get-tuple-element.7.refs_3_), custom_call_target="tpu_custom_call" | custom-call | tf_op jit(solution)/shard_map/solve/pallas_call | solution.py:106
  134.4 10.8 %fusion.9 = f32[4096,128]{1,0:T(8,128)} fusion(bf16[1024,128]{1,0:T(8,128)(2,1)S(1)} %solve.1, f32[1024]{0:T(1024)S(1)} %get-tuple-element.3, bf16[4096,512]{1,0:T(8,128)(2,1)} %param.5, f32[4096]{0:T(1024)S(1)} %get-tuple-element.15, f32[4096]{0:T(1024)S(1)} %broadcast_multiply_fusion, f32[4096,512]{1,0:T(8,128)} %convert_element_type.151, ...), kind=kOutput, calls=%fused_computation.9 | convolution fusion | flops 5399117824 | bytes 9752580 | tf_op jit(solution)/shard_map/dot_general | solution.py:164
  (7 shorter events, 0.1 us)
Async XLA Ops:
  7.2 64.4 %all-gather.2.cloned.1.call-start = ((), (), s32[]{:S(2)}) async-start(), calls=%async_computation | async-start | bytes 2433024 | tf_op jit(solution)/shard_map/all_gather | solution.py:142
Sparse Core Ops, SparseCore 0:
  13.8 57.7 all-gather.1
where the time goes:
time: 154 us; the launch traced here: 153 us
  Pallas kernels  55.7 us (36%)
  waiting for transfers between devices  45 us (29%)
  other arithmetic  22.1 us (14%)
  between operations  15.9 us (10%)
  matrix products  10.8 us (7%)
  local copies, waits for them, and re-layouts  3.56 us (2%)
    pallas_call x1, Pallas kernels, solve(): pl.pallas_call(lambda *refs: solve_kernel(8 * ne, *refs), out_shape=jax.S...  55.7 us
    all_gather x1, waiting for transfers between devices, per_device(): whole = lax.all_gather(payload, ('cell', 'dp'), axis=0, tiled=True)  45 us
    dot_general x1, matrix products, per_device(): increment = jnp.dot(weighted, carried, preferred_element_type=F32)  10.8 us
    convert_element_type x1, other arithmetic, per_device(): values = ensemble.astype(F32)  6.61 us
    reduce_sum x1, other arithmetic, per_device(): mismatch = jnp.sum(joined(parts, 6)) / (nd * ne)  4.21 us
    reduce_sum x1, other arithmetic, per_device(): cell_scale = jnp.sqrt(jnp.mean(anomaly * anomaly, axis=1) + 1e-06)  3.4 us
  transfers between devices with their start and end apart: 1, of which 1 were waited for; matrix products, arithmetic and copies ran while one was open for 8% of the time, Pallas kernels for 0%

commit v1 on v0

--- a/solution.py
+++ b/solution.py
@@ -122,6 +122,163 @@
     )(unit, innovation, ratio, carry)
 
 
+def gather_kernel(nz, ny, nx, unit_in, inn_in, unit_out, inn_out, held, send, recv, local):
+    cores = 2
+    cell, dp = lax.axis_index("cell"), lax.axis_index("dp")
+    z, y = cell // ny, cell % ny
+    x, core = dp // cores, dp % cores
+
+    def z_peer(d):
+        return (((z + d) % nz) * ny + y, dp)
+
+    def x_peer(d):
+        return (cell, ((x + d) % nx) * cores + core)
+
+    def y_peer(d):
+        return (z * ny + (y + d) % ny, dp)
+
+    core_peer = (cell, x * cores + (core + 1) % cores)
+    peers = [z_peer(d) for d in range(1, nz)] + [x_peer(d) for d in range(1, nx)]
+    peers += [y_peer(d) for d in range(1, ny)] + [core_peer]
+    barrier = pltpu.get_barrier_semaphore()
+    for peer in peers:
+        pl.semaphore_signal(
+            barrier, inc=1, device_id=peer, device_id_type=pl.DeviceIdType.MESH
+        )
+    pl.semaphore_wait(barrier, len(peers))
+
+    started = []
+
+    def put(src, dst, peer):
+        at = len(started)
+        copy = pltpu.make_async_remote_copy(
+            src_ref=src,
+            dst_ref=dst,
+            send_sem=send.at[at],
+            recv_sem=recv.at[at],
+            device_id=peer,
+            device_id_type=pl.DeviceIdType.MESH,
+        )
+        copy.start()
+        started.append(copy)
+        return copy
+
+    def own(slot):
+        return all(k == 0 for k in slot)
+
+    def unit_at(slot):
+        return unit_in if own(slot) else unit_out.at[slot]
+
+    def inn_at(slot, *part):
+        if own(slot):
+            return inn_in.at[part] if part else inn_in
+        return held.at[slot + part]
+
+    landed = {}
+
+    def from_z(d):
+        slot = (0, 0, 0, nz - d)
+        landed[slot] = [
+            put(unit_in, unit_out.at[slot], z_peer(d)),
+            put(inn_in, held.at[slot], z_peer(d)),
+        ]
+
+    def along_x(kz):
+        for d in range(1, nx):
+            source, slot = (0, 0, 0, kz), (0, 0, nx - d, kz)
+            landed[slot] = [
+                put(unit_at(source), unit_out.at[slot], x_peer(d)),
+                put(inn_at(source, d), held.at[slot + (0,)], x_peer(d)),
+            ]
+
+    def along_y(kx, kz):
+        for d in range(1, ny):
+            source, slot = (0, 0, kx, kz), (0, ny - d, kx, kz)
+            landed[slot] = [
+                put(unit_at(source), unit_out.at[slot], y_peer(d)),
+                put(inn_at(source, 0), held.at[slot + (0,)], y_peer(d)),
+            ]
+
+    def to_core(ky, kx, kz):
+        source, slot = (0, ky, kx, kz), (1, ky, kx, kz)
+        landed[slot] = [
+            put(unit_at(source), unit_out.at[slot], core_peer),
+            put(inn_at(source, 0, 1), held.at[slot + (0, 0)], core_peer),
+        ]
+
+    def arrived(slot):
+        if not own(slot):
+            for copy in landed[slot]:
+                copy.wait_recv()
+
+    keep = [
+        pltpu.make_async_copy(unit_in, unit_out.at[0, 0, 0, 0], local.at[0]),
+        pltpu.make_async_copy(inn_in, held.at[0, 0, 0, 0], local.at[1]),
+    ]
+    for d in range(1, nz):
+        from_z(d)
+    for copy in keep:
+        copy.start()
+    for kz in range(nz):
+        arrived((0, 0, 0, kz))
+        along_x(kz)
+        along_y(0, kz)
+        to_core(0, 0, kz)
+    for kx in range(1, nx):
+        for kz in range(nz):
+            arrived((0, 0, kx, kz))
+            along_y(kx, kz)
+            to_core(0, kx, kz)
+    for ky in range(1, ny):
+        for kx in range(nx):
+            for kz in range(nz):
+                arrived((0, ky, kx, kz))
+                to_core(ky, kx, kz)
+    for ky in range(ny):
+        for kx in range(nx):
+            for kz in range(nz):
+                arrived((1, ky, kx, kz))
+    for copy in keep:
+        copy.wait()
+    for copy in started:
+        copy.wait_send()
+    for c in range(cores):
+        for ky in range(ny):
+            for kx in range(nx):
+                for kz in range(nz):
+                    inn_out[c, ky, kx, kz] = held[c, ky, kx, kz, 0, 0]
+
+
+def gather(unit, innovation):
+    cells, dps = lax.axis_size("cell"), lax.axis_size("dp")
+    ny = 2 if cells % 2 == 0 else 1
+    nz, nx = cells // ny, dps // 2
+    rows, width = unit.shape
+    cols = innovation.shape[-1]
+    copies = 2 * (cells * dps - 1)
+    vmem = pl.BlockSpec(memory_space=pltpu.VMEM)
+    units, inns = pl.pallas_call(
+        lambda *refs: gather_kernel(nz, ny, nx, *refs),
+        out_shape=[
+            jax.ShapeDtypeStruct((2, ny, nx, nz, rows, width), BF16),
+            jax.ShapeDtypeStruct((2, ny, nx, nz, rows, cols), BF16),
+        ],
+        in_specs=[vmem] * 2,
+        out_specs=[vmem] * 2,
+        scratch_shapes=[
+            pltpu.VMEM((2, ny, nx, nz, nx, 2, rows, cols), BF16),
+            pltpu.SemaphoreType.DMA((copies,)),
+            pltpu.SemaphoreType.DMA((copies,)),
+            pltpu.SemaphoreType.DMA((2,)),
+        ],
+        compiler_params=pltpu.CompilerParams(
+            collective_id=0, has_side_effects=True, vmem_limit_bytes=40 * 2**20
+        ),
+        name="gather",
+    )(unit, innovation)
+    return units.reshape(-1, width), inns.reshape(-1, cols)
+
+
 def per_device(ensemble, response_estimates, observed, obs_std, threshold):
     ne = ensemble.shape[1]
     forecast = response_estimates[0]
@@ -138,14 +295,19 @@
         pieces(ratio) + pieces(carry) + pieces(squares) + [threshold[0].astype(BF16)], axis=1
     )
     meta = jnp.pad(meta, ((0, 0), (0, LANES - meta.shape[1])))
-    payload = jnp.concatenate([unit_data, innovation.astype(BF16), meta], axis=1)
-    whole = lax.all_gather(payload, ("cell", "dp"), axis=0, tiled=True)
+    column_count = ne // lax.axis_size("dp")
+    dp = lax.axis_index("dp")
+    first_col = dp * column_count
+    nx = lax.axis_size("dp") // 2
+    blocks = innovation.astype(BF16).reshape(-1, nx, 2, column_count).transpose(1, 2, 0, 3)
+    blocks = jnp.concatenate([blocks, blocks], axis=0)
+    blocks = lax.dynamic_slice_in_dim(blocks, dp // 2, nx, 0)
+    blocks = jnp.concatenate([blocks, blocks], axis=1)
+    blocks = lax.dynamic_slice_in_dim(blocks, dp % 2, 2, 1)
+    whole, own_innovation = gather(jnp.concatenate([unit_data, meta], axis=1), blocks)
     nd = whole.shape[0]
-    column_count = ne // lax.axis_size("dp")
-    first_col = lax.axis_index("dp") * column_count
     unit_all = whole[:, :ne]
-    own_innovation = lax.dynamic_slice_in_dim(whole, ne + first_col, column_count, 1)
-    parts = whole[:, 2 * ne :]
+    parts = whole[:, ne:]
     mismatch = jnp.sum(joined(parts, 6)) / (nd * ne)
     carried = solve(
         unit_all, own_innovation, joined(parts, 0)[:, None], joined(parts, 3)[:, None]

time: 154 us -> 106 us (0.69)
  waiting for transfers between devices: 45 us -> 0 us
  Pallas kernels: 55.7 us -> 71.9 us
  between operations: 15.9 us -> 2.63 us
  other arithmetic: 22.1 us -> 15.4 us
    all_gather x1 -> x0, waiting for transfers between devices: 45 us -> none  [per_device(): whole = lax.all_gather(payload, ('cell', 'dp'), axis=0, tiled=True)]
    pallas_call x0 -> x1, Pallas kernels: none -> 23.2 us  [gather(): pl.pallas_call(lambda *refs: gather_kernel(nz, ny, nx, *refs), out_shape=...]
    pallas_call x1, Pallas kernels: 55.7 us -> 48.7 us  [solve(): pl.pallas_call(lambda *refs: solve_kernel(8 * ne, *refs), out_shape=jax.S...]
    reduce_sum x1, other arithmetic: 4.21 us -> 1.27 us  [per_device(): mismatch = jnp.sum(joined(parts, 6)) / (nd * ne)]
    unnamed x0 -> x14, local copies, waits for them, and re-layouts: none -> 2.36 us
    reduce_sum x2 -> x0, other arithmetic: 1.98 us -> none  [the longest x1 1.03 us: per_device(): data_scale = jnp.sqrt(jnp.mean(deviation * deviation, axis=1) + 1e-06)]
  transfers between devices with their start and end apart: 1 -> 0, of which waited for: 1 -> 0; matrix products, arithmetic and copies ran while one was open for 8% -> 0% of each run, Pallas kernels for 0% -> 0%
where the time goes in v1:
time: 106 us; the launch traced here: 104 us
  Pallas kernels  71.9 us (68%)
  other arithmetic  15.4 us (15%)
  matrix products  10.5 us (10%)
  local copies, waits for them, and re-layouts  3.76 us (4%)
  between operations  2.63 us (2%)
    pallas_call x1, Pallas kernels, solve(): pl.pallas_call(lambda *refs: solve_kernel(8 * ne, *refs), out_shape=jax.S...  48.7 us
    pallas_call x1, Pallas kernels, gather(): pl.pallas_call(lambda *refs: gather_kernel(nz, ny, nx, *refs), out_shape=...  23.2 us
    dot_general x1, matrix products, per_device(): increment = jnp.dot(weighted, carried, preferred_element_type=F32)  10.5 us
    convert_element_type x1, other arithmetic, per_device(): values = ensemble.astype(F32)  6.65 us
    reduce_sum x1, other arithmetic, per_device(): cell_scale = jnp.sqrt(jnp.mean(anomaly * anomaly, axis=1) + 1e-06)  3.37 us
    reduce_sum x1, other arithmetic, per_device(): anomaly = values - jnp.mean(values, axis=1, keepdims=True)  2.82 us
    unnamed x14, local copies, waits for them, and re-layouts  2.36 us

profile of v1, /device:TPU:11, one launch (start us, length us, event | category | flops | bytes accessed | tf_op | source)
XLA Modules:
  0.0 104.1 jit_solution(13230329171028614446)
XLA Ops:
  0.6 0.0 copy-start.4
  0.6 0.0 copy-start.6
  0.7 0.0 copy-start.5
  0.7 0.7 multiply_bitcast_fusion.1
  1.4 0.7 copy.30
  2.1 0.1 copy.24
  2.2 2.8 %convert_reduce_fusion = f32[4096]{0:T(1024)S(1)} fusion(bf16[4096,512]{1,0:T(8,128)(2,1)} %param.5), kind=kLoop, calls=%fused_computation.7 | loop fusion | flops 4190208 | bytes 4210688 | tf_op jit(solution)/shard_map/reduce_sum | solution.py:318
  5.0 3.4 %multiply_reduce_fusion = f32[4096]{0:T(1024)S(1)} fusion(bf16[4096,512]{1,0:T(8,128)(2,1)} %param.5, f32[4096]{0:T(1024)S(1)} %broadcast_multiply_fusion), kind=kLoop, calls=%fused_computation.4 | loop fusion | flops 8384512 | bytes 4227072 | tf_op jit(solution)/shard_map/reduce_sum | solution.py:319
  8.4 0.0 copy-done.4
  8.5 0.0 copy-done.5
  8.5 0.1 fusion.34
  8.6 0.1 fusion.22
  8.8 0.2 fusion.18
  9.0 0.0 copy-done.6
  9.0 0.1 copy.25
  9.1 0.1 copy.22
  9.2 0.1 copy.27
  9.3 0.1 copy.28
  9.4 0.1 stack.2
  9.5 0.1 divide_convert_fusion.3
  9.6 23.2 %gather.1 = (bf16[2,2,2,4,32,640]{5,4,3,2,1,0:T(8,128)(2,1)S(1)}, bf16[2,2,2,4,32,128]{5,4,3,2,1,0:T(8,128)(2,1)S(1)}) custom-call(bf16[32,640]{1,0:T(8,128)(2,1)S(1)} %fusion.19.refs_0_, bf16[2,2,32,128]{3,2,1,0:T(8,128)(2,1)S(1)} %fusion.20.refs_1_), custom_call_target="tpu_custom_call" | custom-call | tf_op jit(solution)/shard_map/gather/pallas_call | solution.py:260
  32.8 0.0 copy-start
  32.9 0.7 copy-done
  33.6 0.1 slice.55.refs_0_
  33.6 1.3 %add_reduce_fusion = (f32[]{:T(128)}, f32[1024]{0:T(1024)S(1)}, f32[1024,1]{1,0:T(8,128)S(1)}, f32[1024,1]{1,0:T(8,128)S(1)}) fusion(bf16[1024,640]{1,0:T(8,128)(2,1)S(1)} %bitcast.35), kind=kLoop, calls=%fused_computation.11 | loop fusion | flops 18431 | bytes 32772 | tf_op jit(solution)/shard_map/reduce_sum | solution.py:311
  35.6 0.0 copy-start.1
  35.6 0.9 copy-done.1
  36.5 48.7 %solve.1 = bf16[1024,128]{1,0:T(8,128)(2,1)S(1)} custom-call(bf16[1024,512]{1,0:T(8,128)(2,1)S(1)} %slice.55.refs_0_, bf16[1024,128]{1,0:T(8,128)(2,1)S(1)} %bitcast.37, f32[1024,1]{1,0:T(8,128)S(1)} %get-tuple-element.10.refs_2_, f32[1024,1]{1,0:T(8,128)S(1)} %get-tuple-element.11.refs_3_), custom_call_target="tpu_custom_call" | custom-call | tf_op jit(solution)/shard_map/solve/pallas_call | solution.py:106
  85.2 0.0 copy-start.2
  85.2 0.7 copy-done.2
  85.9 6.7 %convert_element_type.152 = f32[4096,512]{1,0:T(8,128)} convert(bf16[4096,512]{1,0:T(8,128)(2,1)} %param.5) | non-fusion elementwise | flops 2097152 | bytes 12582912 | tf_op jit(solution)/shard_map/convert_element_type | solution.py:317
  92.6 10.5 %fusion.9 = f32[4096,128]{1,0:T(8,128)} fusion(bf16[1024,128]{1,0:T(8,128)(2,1)S(1)} %copy-done.3, f32[1024]{0:T(1024)S(1)} %get-tuple-element.7, bf16[4096,512]{1,0:T(8,128)(2,1)} %param.5, f32[4096]{0:T(1024)S(1)} %get-tuple-element.20, f32[4096]{0:T(1024)S(1)} %broadcast_multiply_fusion, f32[4096,512]{1,0:T(8,128)} %convert_element_type.152, ...), kind=kOutput, calls=%fused_computation.9 | convolution fusion | flops 5399117824 | bytes 9752580 | tf_op jit(solution)/shard_map/dot_general | solution.py:326
  (14 shorter events, 0.2 us)
Async XLA Ops:
  0.6 7.8 %copy-start.4 = (f32[1,32,512]{2,1,0:T(8,128)S(1)}, f32[1,32,512]{2,1,0:T(8,128)}, u32[]{:S(2)}) copy-start(f32[1,32,512]{2,1,0:T(8,128)} %param.6) | copy-start | bytes 196612
  0.6 8.4 %copy-start.6 = (f32[1,32]{1,0:T(1,128)S(1)}, f32[1,32]{1,0:T(1,128)}, u32[]{:S(2)}) copy-start(f32[1,32]{1,0:T(1,128)} %param.8) | copy-start | bytes 388
  0.7 7.8 %copy-start.5 = (f32[1,32,512]{2,1,0:T(8,128)S(1)}, f32[1,32,512]{2,1,0:T(8,128)}, u32[]{:S(2)}) copy-start(f32[1,32,512]{2,1,0:T(8,128)} %param.7) | copy-start | bytes 196612
  32.8 0.7 copy-start
  35.6 1.0 copy-start.1
  85.2 0.7 copy-start.2
  85.9 6.7 %copy-start.3 = (bf16[1024,128]{1,0:T(8,128)(2,1)S(1)}, bf16[1024,128]{1,0:T(8,128)(2,1)}, u32[]{:S(2)}) copy-start(bf16[1024,128]{1,0:T(8,128)(2,1)} %copy-done.2) | copy-start | bytes 786436

commit v2 on v1

--- a/solution.py
+++ b/solution.py
@@ -58,7 +58,7 @@
     inn = innovation[...]
     rhs = tdot(high, inn) + tdot(low, inn)
     inn32 = inn.astype(F32)
-    goal = jnp.sum(inn32 * inn32, axis=0, keepdims=True) * (2.0**-30)
+    goal = jnp.sum(inn32 * inn32, axis=0, keepdims=True) * (2.0**-24)
     x[...] = jnp.zeros_like(x)
     r[...] = rhs
     p[...] = rhs
@@ -279,6 +279,50 @@
     return units.reshape(-1, width), inns.reshape(-1, cols)
 
 
+def taper_kernel(_, ensemble, own, unit, carried, limit2, out):
+    ne = ensemble.shape[1]
+    nd = carried.shape[0]
+    values = ensemble[...].astype(F32)
+    anomaly = values - jnp.mean(values, axis=1, keepdims=True)
+    scale = jnp.sqrt(jnp.mean(anomaly * anomaly, axis=1, keepdims=True) + 1e-06)
+    cells = (anomaly * (1.0 / (scale * math.sqrt(ne)))).astype(BF16)
+    step = 256 if nd % 256 == 0 else nd
+    total = jnp.zeros(out.shape, F32)
+    for first in range(0, nd, step):
+        rows = slice(first, first + step)
+        correlate = lax.dot_general(
+            cells, unit[rows, :ne], (((1,), (1,)), ((), ())), preferred_element_type=F32
+        )
+        square = correlate * correlate
+        weighted = (square / (square + limit2[:, rows]) * correlate).astype(BF16)
+        total = total + jnp.dot(weighted, carried[rows, :], preferred_element_type=F32)
+    out[...] = own[...].astype(F32) + scale * (ne / (ne - 1.0)) * total
+
+
+def taper(dp, ensemble, unit, carried, limit2):
+    rows, ne = ensemble.shape
+    nd, cols = carried.shape
+    block = 512 if rows % 512 == 0 else rows
+    return pl.pallas_call(
+        taper_kernel,
+        grid_spec=pltpu.PrefetchScalarGridSpec(
+            num_scalar_prefetch=1,
+            grid=(rows // block,),
+            in_specs=[
+                pl.BlockSpec((block, ne), lambda i, at: (i, 0)),
+                pl.BlockSpec((block, cols), lambda i, at: (i, at[0])),
+                pl.BlockSpec(unit.shape, lambda i, at: (0, 0)),
+                pl.BlockSpec((nd, cols), lambda i, at: (0, 0)),
+                pl.BlockSpec((1, nd), lambda i, at: (0, 0)),
+            ],
+            out_specs=pl.BlockSpec((block, cols), lambda i, at: (i, 0)),
+        ),
+        out_shape=jax.ShapeDtypeStruct((rows, cols), F32),
+        compiler_params=pltpu.CompilerParams(vmem_limit_bytes=40 * 2**20),
+        name="taper",
+    )(dp.reshape(1).astype(jnp.int32), ensemble, ensemble, unit, carried, limit2)
+
+
 def per_device(ensemble, response_estimates, observed, obs_std, threshold):
     ne = ensemble.shape[1]
     forecast = response_estimates[0]
@@ -297,7 +341,6 @@
     meta = jnp.pad(meta, ((0, 0), (0, LANES - meta.shape[1])))
     column_count = ne // lax.axis_size("dp")
     dp = lax.axis_index("dp")
-    first_col = dp * column_count
     nx = lax.axis_size("dp") // 2
     blocks = innovation.astype(BF16).reshape(-1, nx, 2, column_count).transpose(1, 2, 0, 3)
     blocks = jnp.concatenate([blocks, blocks], axis=0)
@@ -314,18 +357,7 @@
     )
     limit = parts[:, 9].astype(F32)
 
-    values = ensemble.astype(F32)
-    anomaly = values - jnp.mean(values, axis=1, keepdims=True)
-    cell_scale = jnp.sqrt(jnp.mean(anomaly * anomaly, axis=1) + 1e-06)
-    unit_cells = (anomaly / (cell_scale[:, None] * math.sqrt(ne))).astype(BF16)
-    correlate = lax.dot_general(
-        unit_cells, unit_all, (((1,), (1,)), ((), ())), preferred_element_type=F32
-    )
-    square = correlate * correlate
-    weighted = (square / (square + (limit * limit)[None, :]) * correlate).astype(BF16)
-    increment = jnp.dot(weighted, carried, preferred_element_type=F32)
-    own_values = lax.dynamic_slice_in_dim(values, first_col, column_count, 1)
-    updated = own_values + cell_scale[:, None] * (ne / (ne - 1.0)) * increment
+    updated = taper(dp, ensemble, whole, carried, (limit * limit)[None, :])
     return (updated, mismatch)
 
 

time: 106 us -> 92.5 us (0.87); the launches traced: 104 us -> 92.1 us
  matrix products: 10.5 us -> 0 us
  other arithmetic: 15.4 us -> 5.79 us
  Pallas kernels: 71.9 us -> 79.2 us
    pallas_call x0 -> x1, Pallas kernels: none -> 12.3 us  [taper(): pl.pallas_call(taper_kernel, grid_spec=pltpu.PrefetchScalarGridSpec(num_s...]
    dot_general x1 -> x0, matrix products: 10.5 us -> none  [per_device(): increment = jnp.dot(weighted, carried, preferred_element_type=F32)]
    convert_element_type x1 -> x0, other arithmetic: 6.65 us -> none  [per_device(): values = ensemble.astype(F32)]
    reduce_sum x2 -> x0, other arithmetic: 6.19 us -> none  [the longest x1 3.37 us: per_device(): cell_scale = jnp.sqrt(jnp.mean(anomaly * anomaly, axis=1) + 1e-06)]
    pallas_call x1, Pallas kernels: 48.7 us -> 43.7 us  [solve(): pl.pallas_call(lambda *refs: solve_kernel(8 * ne, *refs), out_shape=jax.S...]
    unnamed x14 -> x6, local copies, waits for them, and re-layouts: 2.36 us -> 3.13 us
where the time goes in v2:
time: 92.5 us; the launch traced here: 92.1 us
  Pallas kernels  79.2 us (86%)
  other arithmetic  5.79 us (6%)
  local copies, waits for them, and re-layouts  4.55 us (5%)
  between operations  2.55 us (3%)
    pallas_call x1, Pallas kernels, solve(): pl.pallas_call(lambda *refs: solve_kernel(8 * ne, *refs), out_shape=jax.S...  43.7 us
    pallas_call x1, Pallas kernels, gather(): pl.pallas_call(lambda *refs: gather_kernel(nz, ny, nx, *refs), out_shape=...  23.2 us
    pallas_call x1, Pallas kernels, taper(): pl.pallas_call(taper_kernel, grid_spec=pltpu.PrefetchScalarGridSpec(num_s...  12.3 us
    unnamed x6, local copies, waits for them, and re-layouts  3.13 us

profile of v2, /device:TPU:11, one launch (start us, length us, event | category | flops | bytes accessed | tf_op | source)
XLA Modules:
  0.0 92.1 jit_solution(9025656872375675199)
XLA Ops:
  0.7 0.7 multiply_bitcast_fusion.1
  1.3 0.7 copy.30
  2.1 0.1 copy.24
  2.2 1.0 %fusion.16 = (f32[1,32,512]{2,1,0:T(8,128)S(1)}, f32[32]{0:T(128)S(1)}) fusion(f32[1,32,512]{2,1,0:T(8,128)} %param.7, f32[1,32,512]{2,1,0:T(8,128)} %param.6), kind=kLoop, calls=%fused_computation.48 | loop fusion | flops 32736 | bytes 196736 | tf_op jit(solution)/shard_map/sub | solution.py:336
  3.2 0.1 fusion.8
  3.4 1.1 %fusion.4 = (f32[32]{0:T(128)S(1)}, f32[32]{0:T(128)S(1)}) fusion(f32[1,32,512]{2,1,0:T(8,128)} %param.6, f32[1,32,512]{2,1,0:T(8,128)} %param.7, f32[32]{0:T(128)S(1)} %get-tuple-element.25, f32[32]{0:T(128)S(1)} %broadcast_multiply_fusion.1), kind=kLoop, calls=%fused_computation.18 | loop fusion | flops 114624 | bytes 131584 | tf_op jit(solution)/shard_map/reduce_sum | solution.py:337
  4.4 0.7 bitcast_divide_fusion
  5.1 0.1 copy.25
  5.2 0.1 copy.22
  5.3 0.1 copy.27
  5.4 0.1 copy.28
  5.5 0.1 stack.2
  5.6 0.9 %divide_convert_fusion = bf16[32,512]{1,0:T(8,128)(2,1)S(1)} fusion(f32[1,32,512]{2,1,0:T(8,128)} %param.6, f32[32]{0:T(128)S(1)} %get-tuple-element.23, f32[32]{0:T(128)S(1)} %broadcast_multiply_fusion.1), kind=kLoop, calls=%fused_computation.16 | loop fusion | flops 49152 | bytes 98560 | tf_op jit(solution)/shard_map/convert_element_type | solution.py:333
  6.6 23.2 %gather.1 = (bf16[2,2,2,4,32,640]{5,4,3,2,1,0:T(8,128)(2,1)S(1)}, bf16[2,2,2,4,32,128]{5,4,3,2,1,0:T(8,128)(2,1)S(1)}) custom-call(bf16[32,640]{1,0:T(8,128)(2,1)S(1)} %fusion.5.refs_0_, bf16[2,2,32,128]{3,2,1,0:T(8,128)(2,1)S(1)} %fusion.6.refs_1_), custom_call_target="tpu_custom_call" | custom-call | tf_op jit(solution)/shard_map/gather/pallas_call | solution.py:260
  29.8 0.0 copy-start.1
  29.8 0.1 slice.55.refs_0_
  29.9 1.3 %add_reduce_fusion = (f32[]{:T(128)}, f32[1024]{0:T(1024)S(1)}, f32[1024,1]{1,0:T(8,128)S(1)}, f32[1024,1]{1,0:T(8,128)S(1)}) fusion(bf16[1024,640]{1,0:T(8,128)(2,1)S(1)} %bitcast.36), kind=kLoop, calls=%fused_computation | loop fusion | flops 18431 | bytes 32772 | tf_op jit(solution)/shard_map/reduce_sum | solution.py:354
  31.1 0.0 copy-done.1
  31.8 0.0 copy-start.2
  31.8 0.9 %copy-done.2 = bf16[2,2,2,4,32,128]{5,4,3,2,1,0:T(8,128)(2,1)S(1)} copy-done((bf16[2,2,2,4,32,128]{5,4,3,2,1,0:T(8,128)(2,1)S(1)}, bf16[2,2,2,4,32,128]{5,4,3,2,1,0:T(8,128)(2,1)}, u32[]{:S(2)}) %copy-start.2) | copy-done | bytes 262168
  32.8 43.7 %solve.1.carried = bf16[1024,128]{1,0:T(8,128)(2,1)S(1)} custom-call(bf16[1024,512]{1,0:T(8,128)(2,1)S(1)} %slice.55.refs_0_, bf16[1024,128]{1,0:T(8,128)(2,1)S(1)} %bitcast.38, f32[1024,1]{1,0:T(8,128)S(1)} %get-tuple-element.10.refs_2_, f32[1024,1]{1,0:T(8,128)S(1)} %get-tuple-element.11.refs_3_), custom_call_target="tpu_custom_call" | custom-call | tf_op jit(solution)/shard_map/solve/pallas_call | solution.py:106
  76.5 0.0 copy-start
  76.5 2.2 %copy-done = bf16[4096,512]{1,0:T(8,128)(2,1)S(1)} copy-done((bf16[4096,512]{1,0:T(8,128)(2,1)S(1)}, bf16[4096,512]{1,0:T(8,128)(2,1)}, u32[]{:S(2)}) %copy-start) | copy-done | bytes 4194328
  78.7 12.3 %taper.1 = f32[4096,128]{1,0:T(8,128)} custom-call(s32[1]{0:T(128)} %bitcast._, bf16[4096,512]{1,0:T(8,128)(2,1)S(1)} %copy-done, bf16[4096,512]{1,0:T(8,128)(2,1)S(1)} %copy-done, bf16[1024,640]{1,0:T(8,128)(2,1)S(1)} %bitcast.37, bf16[1024,128]{1,0:T(8,128)(2,1)S(1)} %solve.1.carried, f32[1,1024]{1,0:T(1,128)S(1)} %bitcast.39), custom_call_target="tpu_custom_call" | custom-call | tf_op jit(solution)/shard_map/taper/pallas_call | solution.py:306
  (9 shorter events, 0.2 us)
Async XLA Ops:
  29.8 1.4 %copy-start.1 = (bf16[2,2,2,4,32,128]{5,4,3,2,1,0:T(8,128)(2,1)}, bf16[2,2,2,4,32,128]{5,4,3,2,1,0:T(8,128)(2,1)S(1)}, u32[]{:S(2)}) copy-start(bf16[2,2,2,4,32,128]{5,4,3,2,1,0:T(8,128)(2,1)S(1)} %get-tuple-element.5) | copy-start | bytes 786436
  31.8 1.0 %copy-start.2 = (bf16[2,2,2,4,32,128]{5,4,3,2,1,0:T(8,128)(2,1)S(1)}, bf16[2,2,2,4,32,128]{5,4,3,2,1,0:T(8,128)(2,1)}, u32[]{:S(2)}) copy-start(bf16[2,2,2,4,32,128]{5,4,3,2,1,0:T(8,128)(2,1)} %copy-done.1) | copy-start | bytes 786436
  76.5 2.2 %copy-start = (bf16[4096,512]{1,0:T(8,128)(2,1)S(1)}, bf16[4096,512]{1,0:T(8,128)(2,1)}, u32[]{:S(2)}) copy-start(bf16[4096,512]{1,0:T(8,128)(2,1)} %own.1) | copy-start | bytes 12582916

commit v3 on v2

--- a/solution.py
+++ b/solution.py
@@ -59,40 +59,57 @@
     rhs = tdot(high, inn) + tdot(low, inn)
     inn32 = inn.astype(F32)
     goal = jnp.sum(inn32 * inn32, axis=0, keepdims=True) * (2.0**-24)
+    rr0 = jnp.sum(rhs * rhs, axis=0, keepdims=True)
+
+    def coarse(v):
+        return jnp.dot(a2[:ne, :], v.astype(BF16), preferred_element_type=F32)
+
+    def full(v):
+        v_high, v_low = split2(v)
+        both = jnp.dot(
+            a2[:ne, :], jnp.concatenate([v_high, v_low], axis=1), preferred_element_type=F32
+        )
+        return (both[:, :cols] + both[:, cols:]) + jnp.dot(
+            a2[ne:, :], v_high, preferred_element_type=F32
+        )
+
+    def run(operator, residual, rr_first, bound, limit):
+        r[...] = residual
+        p[...] = residual
+        norms[0:1, :] = rr_first
+        norms[1:2, :] = bound
+
+        def more(state):
+            step, worst = state
+            return jnp.logical_and(step < limit, worst > 0.0)
+
+        def block(state):
+            step, _ = state
+            rr = norms[0:1, :]
+            for _ in range(CHECK_EVERY):
+                p_now = p[...]
+                q = operator(p_now)
+                pq = jnp.sum(p_now * q, axis=0, keepdims=True)
+                alpha = jnp.where(pq > 0.0, rr / jnp.where(pq > 0.0, pq, 1.0), 0.0)
+                x[...] = x[...] + alpha * p_now
+                r_new = r[...] - alpha * q
+                r[...] = r_new
+                rr_new = jnp.sum(r_new * r_new, axis=0, keepdims=True)
+                beta = jnp.where(rr > 0.0, rr_new / jnp.where(rr > 0.0, rr, 1.0), 0.0)
+                p[...] = r_new + beta * p_now
+                rr = rr_new
+            norms[0:1, :] = rr
+            return step + CHECK_EVERY, jnp.max(rr - norms[1:2, :])
+
+        lax.while_loop(more, block, (jnp.int32(0), jnp.max(rr_first - bound)))
+
     x[...] = jnp.zeros_like(x)
-    r[...] = rhs
-    p[...] = rhs
-    rr0 = jnp.sum(rhs * rhs, axis=0, keepdims=True)
-    norms[0:1, :] = rr0
-    norms[1:2, :] = goal
-
-    def more(state):
-        step, worst = state
-        return jnp.logical_and(step < limit_steps, worst > 0.0)
-
-    def block(state):
-        step, _ = state
-        rr = norms[0:1, :]
-        for _ in range(CHECK_EVERY):
-            p_now = p[...]
-            p_high, p_low = split2(p_now)
-            both = jnp.dot(
-                a2[...], jnp.concatenate([p_high, p_low], axis=1), preferred_element_type=F32
-            )
-            q = (both[:ne, :cols] + both[:ne, cols:]) + (both[ne:, :cols] + both[ne:, cols:])
-            pq = jnp.sum(p_now * q, axis=0, keepdims=True)
-            alpha = jnp.where(pq > 0.0, rr / jnp.where(pq > 0.0, pq, 1.0), 0.0)
-            x[...] = x[...] + alpha * p_now
-            r_new = r[...] - alpha * q
-            r[...] = r_new
-            rr_new = jnp.sum(r_new * r_new, axis=0, keepdims=True)
-            beta = jnp.where(rr > 0.0, rr_new / jnp.where(rr > 0.0, rr, 1.0), 0.0)
-            p[...] = r_new + beta * p_now
-            rr = rr_new
-        norms[0:1, :] = rr
-        return step + CHECK_EVERY, jnp.max(rr - norms[1:2, :])
-
-    lax.while_loop(more, block, (jnp.int32(0), jnp.max(rr0 - goal)))
+    run(coarse, rhs, rr0, goal * (2.0**12), min(24, limit_steps))
+    left = rhs - full(x[...])
+    rr1 = jnp.sum(left * left, axis=0, keepdims=True)
+    useful = rr1 < rr0
+    x[...] = jnp.where(useful, x[...], 0.0)
+    run(full, jnp.where(useful, left, rhs), jnp.where(useful, rr1, rr0), goal, limit_steps)
     x_high, x_low = split2(x[...])
     both = jnp.dot(s2[...], jnp.concatenate([x_high, x_low], axis=1), preferred_element_type=F32)
     fitted = (both[:nd, :cols] + both[:nd, cols:]) + (both[nd:, :cols] + both[nd:, cols:])

time: 92.5 us -> 86.5 us (0.935); the launches traced: 92.1 us -> 88.1 us
  Pallas kernels: 79.2 us -> 75.2 us
    pallas_call x1, Pallas kernels: 43.7 us -> 39.6 us  [solve(): pl.pallas_call(lambda *refs: solve_kernel(8 * ne, *refs), out_shape=jax.S...]
where the time goes in v3:
time: 86.5 us; the launch traced here: 88.1 us
  Pallas kernels  75.2 us (87%)
  other arithmetic  5.79 us (7%)
  local copies, waits for them, and re-layouts  4.55 us (5%)
  between operations  2.55 us (3%)
    pallas_call x1, Pallas kernels, solve(): pl.pallas_call(lambda *refs: solve_kernel(8 * ne, *refs), out_shape=jax.S...  39.6 us
    pallas_call x1, Pallas kernels, gather(): pl.pallas_call(lambda *refs: gather_kernel(nz, ny, nx, *refs), out_shape=...  23.2 us
    pallas_call x1, Pallas kernels, taper(): pl.pallas_call(taper_kernel, grid_spec=pltpu.PrefetchScalarGridSpec(num_s...  12.3 us
    unnamed x6, local copies, waits for them, and re-layouts  3.13 us

profile of v3, /device:TPU:11, one launch (start us, length us, event | category | flops | bytes accessed | tf_op | source)
XLA Modules:
  0.0 88.1 jit_solution(4980190392891661595)
XLA Ops:
  0.7 0.7 multiply_bitcast_fusion.1
  1.3 0.7 copy.30
  2.1 0.1 copy.24
  2.2 1.0 %fusion.16 = (f32[1,32,512]{2,1,0:T(8,128)S(1)}, f32[32]{0:T(128)S(1)}) fusion(f32[1,32,512]{2,1,0:T(8,128)} %param.7, f32[1,32,512]{2,1,0:T(8,128)} %param.6), kind=kLoop, calls=%fused_computation.48 | loop fusion | flops 32736 | bytes 196736 | tf_op jit(solution)/shard_map/sub | solution.py:353
  3.2 0.1 fusion.8
  3.4 1.1 %fusion.4 = (f32[32]{0:T(128)S(1)}, f32[32]{0:T(128)S(1)}) fusion(f32[1,32,512]{2,1,0:T(8,128)} %param.6, f32[1,32,512]{2,1,0:T(8,128)} %param.7, f32[32]{0:T(128)S(1)} %get-tuple-element.25, f32[32]{0:T(128)S(1)} %broadcast_multiply_fusion.1), kind=kLoop, calls=%fused_computation.18 | loop fusion | flops 114624 | bytes 131584 | tf_op jit(solution)/shard_map/reduce_sum | solution.py:354
  4.4 0.7 bitcast_divide_fusion
  5.1 0.1 copy.25
  5.2 0.1 copy.22
  5.3 0.1 copy.27
  5.4 0.1 copy.28
  5.5 0.1 stack.2
  5.6 0.9 %divide_convert_fusion = bf16[32,512]{1,0:T(8,128)(2,1)S(1)} fusion(f32[1,32,512]{2,1,0:T(8,128)} %param.6, f32[32]{0:T(128)S(1)} %get-tuple-element.23, f32[32]{0:T(128)S(1)} %broadcast_multiply_fusion.1), kind=kLoop, calls=%fused_computation.16 | loop fusion | flops 49152 | bytes 98560 | tf_op jit(solution)/shard_map/convert_element_type | solution.py:350
  6.6 23.2 %gather.1 = (bf16[2,2,2,4,32,640]{5,4,3,2,1,0:T(8,128)(2,1)S(1)}, bf16[2,2,2,4,32,128]{5,4,3,2,1,0:T(8,128)(2,1)S(1)}) custom-call(bf16[32,640]{1,0:T(8,128)(2,1)S(1)} %fusion.5.refs_0_, bf16[2,2,32,128]{3,2,1,0:T(8,128)(2,1)S(1)} %fusion.6.refs_1_), custom_call_target="tpu_custom_call" | custom-call | tf_op jit(solution)/shard_map/gather/pallas_call | solution.py:277
  29.8 0.0 copy-start.1
  29.8 0.1 slice.55.refs_0_
  29.9 1.3 %add_reduce_fusion = (f32[]{:T(128)}, f32[1024]{0:T(1024)S(1)}, f32[1024,1]{1,0:T(8,128)S(1)}, f32[1024,1]{1,0:T(8,128)S(1)}) fusion(bf16[1024,640]{1,0:T(8,128)(2,1)S(1)} %bitcast.36), kind=kLoop, calls=%fused_computation | loop fusion | flops 18431 | bytes 32772 | tf_op jit(solution)/shard_map/reduce_sum | solution.py:371
  31.1 0.0 copy-done.1
  31.8 0.0 copy-start.2
  31.8 0.9 %copy-done.2 = bf16[2,2,2,4,32,128]{5,4,3,2,1,0:T(8,128)(2,1)S(1)} copy-done((bf16[2,2,2,4,32,128]{5,4,3,2,1,0:T(8,128)(2,1)S(1)}, bf16[2,2,2,4,32,128]{5,4,3,2,1,0:T(8,128)(2,1)}, u32[]{:S(2)}) %copy-start.2) | copy-done | bytes 262168
  32.8 39.6 %solve.1.carried = bf16[1024,128]{1,0:T(8,128)(2,1)S(1)} custom-call(bf16[1024,512]{1,0:T(8,128)(2,1)S(1)} %slice.55.refs_0_, bf16[1024,128]{1,0:T(8,128)(2,1)S(1)} %bitcast.38, f32[1024,1]{1,0:T(8,128)S(1)} %get-tuple-element.10.refs_2_, f32[1024,1]{1,0:T(8,128)S(1)} %get-tuple-element.11.refs_3_), custom_call_target="tpu_custom_call" | custom-call | tf_op jit(solution)/shard_map/solve/pallas_call | solution.py:123
  72.4 0.0 copy-start
  72.4 2.2 %copy-done = bf16[4096,512]{1,0:T(8,128)(2,1)S(1)} copy-done((bf16[4096,512]{1,0:T(8,128)(2,1)S(1)}, bf16[4096,512]{1,0:T(8,128)(2,1)}, u32[]{:S(2)}) %copy-start) | copy-done | bytes 4194328
  74.6 12.3 %taper.1 = f32[4096,128]{1,0:T(8,128)} custom-call(s32[1]{0:T(128)} %bitcast._, bf16[4096,512]{1,0:T(8,128)(2,1)S(1)} %copy-done, bf16[4096,512]{1,0:T(8,128)(2,1)S(1)} %copy-done, bf16[1024,640]{1,0:T(8,128)(2,1)S(1)} %bitcast.37, bf16[1024,128]{1,0:T(8,128)(2,1)S(1)} %solve.1.carried, f32[1,1024]{1,0:T(1,128)S(1)} %bitcast.39), custom_call_target="tpu_custom_call" | custom-call | tf_op jit(solution)/shard_map/taper/pallas_call | solution.py:323
  (9 shorter events, 0.2 us)
Async XLA Ops:
  29.8 1.4 %copy-start.1 = (bf16[2,2,2,4,32,128]{5,4,3,2,1,0:T(8,128)(2,1)}, bf16[2,2,2,4,32,128]{5,4,3,2,1,0:T(8,128)(2,1)S(1)}, u32[]{:S(2)}) copy-start(bf16[2,2,2,4,32,128]{5,4,3,2,1,0:T(8,128)(2,1)S(1)} %get-tuple-element.5) | copy-start | bytes 786436
  31.8 1.0 %copy-start.2 = (bf16[2,2,2,4,32,128]{5,4,3,2,1,0:T(8,128)(2,1)S(1)}, bf16[2,2,2,4,32,128]{5,4,3,2,1,0:T(8,128)(2,1)}, u32[]{:S(2)}) copy-start(bf16[2,2,2,4,32,128]{5,4,3,2,1,0:T(8,128)(2,1)} %copy-done.1) | copy-start | bytes 786436
  72.4 2.2 %copy-start = (bf16[4096,512]{1,0:T(8,128)(2,1)S(1)}, bf16[4096,512]{1,0:T(8,128)(2,1)}, u32[]{:S(2)}) copy-start(bf16[4096,512]{1,0:T(8,128)(2,1)} %own.1) | copy-start | bytes 12582916
